TPU v7x, 256 devices: a whole 4x4x8 slice. The times are simulated.
256 devices in a mesh: slab: 64 (over y, z, core), grp: 4 (over x).
Axes of the slice: x: 4, y: 4, z: 8, core: 2. Of those that a mesh axis runs over, the one named last changes fastest.
Arguments:
- blocks: bfloat16 [4, 4, 1024, 128, 128], P('grp', None, 'slab'), may hold values from -6 to 6
- coords: int32 [4, 64, 4, 2], P('grp', 'slab'), may hold values from 0 to 15
- counts: int32 [4, 64], P('grp', 'slab'), may hold values from 1 to 4, as said below
- omega1: bfloat16 [1024, 512], replicated, may hold values from -0.1875 to 0.1875
- omega2: bfloat16 [2048, 512], replicated, may hold values from -0.5 to 0.5
- omega3: bfloat16 [2048, 512], replicated, may hold values from -0.125 to 0.125
Outputs:
- core_sketch: float32 [512, 512, 512], P(None, 'slab', 'grp')
Inputs may be any that keep to these rules, and one draw needn't show every extreme that they name: counts[g, s] slots are live in the list of group g on slab s; slots from it on are ignored. Some list holds 4 live slots in every draw.
All inputs are finite; a program needn't handle non-finite values.
Results may differ from a plain program's by a relative error of at most 0.0041.
Values may be sent and summed in bfloat16 or wider, within the bound.
No kernel may reach another device: no remote copies, remote signals or barrier semaphores. Data moves between devices by JAX's collectives and lax.ppermute only.
A program may use at most 128 MiB of HBM per device.

v0:
```python
import jax
import jax.numpy as jnp
from jax import lax
from jax.sharding import PartitionSpec as P


def contract(running, one_block, coordinate, omega2, third_cols):
    block_edge = one_block.shape[-1]
    third_rows = lax.dynamic_slice_in_dim(third_cols, coordinate[1] * block_edge, block_edge, 0)
    second_rows = lax.dynamic_slice_in_dim(omega2, coordinate[0] * block_edge, block_edge, 0)
    after_third = jnp.einsum(
        "iab,bs->ias", one_block, third_rows, preferred_element_type=jnp.float32
    ).astype(jnp.bfloat16)
    return running + jnp.einsum(
        "ias,ar->sir", after_third, second_rows, preferred_element_type=jnp.float32
    )


def local(blocks, coords, counts, omega1, omega2, omega3):
    own_blocks = blocks[0]
    places = coords[0, 0]
    live_count = counts[0, 0]
    slab_depth = own_blocks.shape[1]
    sketch_width = omega2.shape[1]
    empty_sketch = jnp.zeros((omega3.shape[1], slab_depth, sketch_width), jnp.float32)

    def own_step(position, running):
        return contract(running, own_blocks[position], places[position], omega2, omega3)

    sketch = lax.fori_loop(0, live_count, own_step, empty_sketch)
    reduced = lax.psum_scatter(sketch, "grp", scatter_dimension=0, tiled=True).astype(jnp.bfloat16)
    folded = lax.all_to_all(reduced, "slab", split_axis=2, concat_axis=1, tiled=True)
    return jnp.einsum("ir,sip->rps", omega1, folded, preferred_element_type=jnp.float32)


def solution(mesh):
    in_specs = (
        P("grp", None, "slab", None, None),
        P("grp", "slab", None, None),
        P("grp", "slab"),
        P(),
        P(),
        P(),
    )
    out_specs = P(None, "slab", "grp")
    return jax.shard_map(local, mesh=mesh, in_specs=in_specs, out_specs=out_specs, check_vma=False)
```

profile of v0, /device:TPU:1, one launch (start us, length us, event | category | flops | bytes accessed | tf_op | source)
XLA Modules:
  0.0 328.9 jit_solution(5539492059994773851)
XLA Ops:
  6.5 0.0 copy-start
  6.5 0.0 reduce-scatter.2.cloned.1.call-start
  6.5 0.0 copy-start.1
  6.5 7.9 %broadcast_in_dim.3 = f32[512,16,512]{0,2,1:T(8,128)} broadcast(f32[]{:T(128)} %constant.15.clone.1), dimensions={} | broadcast | bytes 16777220 | tf_op jit(solution)/shard_map/broadcast_in_dim | solution.py:25
  14.4 0.0 copy-done.1
  14.4 17.8 %while.10 = (s32[]{:T(128)}, f32[512,16,512]{0,2,1:T(8,128)}, s32[]{:T(128)}, s32[4,2]{0,1:T(2,128)S(1)}, bf16[2048,512]{1,0:T(8,128)(2,1)}, /*index=5*/bf16[4,1...) while((s32[]{:T(128)}, f32[512,16,512]{0,2,1:T(8,128)}, ...), condition=%wide.region_1.0_spmd, body=%wide.region_0.0_spmd.sunk | while | flops 1347420160 | bytes 34341160 | solution.py:30
  15.1 0.1 constant_dynamic-slice_fusion.2
  15.1 0.5 fusion.31
  16.9 14.6 %bitcast_add_fusion.2 = f32[512,16,512]{0,2,1:T(8,128)} fusion(f32[512,16,512]{0,2,1:T(8,128)} %get-tuple-element.149, bf16[4,16,128,128]{3,2,1,0:T(8,128)(2,1)} %get-tuple-element.165, s32[]{:T(128)S(6)} %select_n.13, bf16[2048,512]{1,0:T(8,128)(2,1)} %get-tuple-element.166, s32[]{:T(128)S(6)} %select_n.14, bf16[2048,512]{1,0:T(8,128)(2,1)} %get-tuple-element.164, ...), kind=kOutput, calls=%fused_computation.clone.1 | convolution fusion | flops 1347420160 | bytes 34340876 | tf_op jit(solution)/shard_map/while/body/ias,ar->sir/dot_general | solution.py:14
  32.2 17.7 %copy.18 = f32[512,16,512]{0,1,2:T(8,128)} copy(f32[512,16,512]{0,2,1:T(8,128)} %get-tuple-element.43) | data formatting | bytes 33554432 | tf_op jit(solution)/shard_map/while | solution.py:30
  49.9 0.0 reduce-scatter.2.cloned.1.call-update
  49.9 204.3 %reduce-scatter.2.cloned.1.call-done = f32[128,16,512]{0,1,2:T(8,128)} async-done(((f32[512,16,512]{0,1,2:T(8,128)}), f32[128,16,512]{0,1,2:T(8,128)}) %reduce-scatter.2.cloned.1.call-update) | async-done | bytes 4194320 | tf_op jit(solution)/shard_map/reduce_scatter | solution.py:31
  254.2 2.5 convert_element_type.6
  256.6 61.7 %all_to_all.18 = bf16[128,16,512]{0,1,2:T(8,128)(2,1)S(1)} all-to-all(bf16[128,16,512]{0,1,2:T(8,128)(2,1)S(1)} %convert_element_type.6), channel_id=1, replica_groups=mesh['slab'=64,'grp'=4] {'slab'}, dimensions={2} | all-to-all | bytes 4194304 | tf_op jit(solution)/shard_map/all_to_all | solution.py:32
  318.4 0.5 copy.20
  318.9 0.0 copy-done
  318.9 1.3 fusion.17
  320.2 1.8 copy.22
Async XLA Ops:
  6.5 312.4 %copy-start = (bf16[1024,512]{1,0:T(8,128)(2,1)S(1)}, bf16[1024,512]{1,0:T(8,128)(2,1)}, u32[]{:S(2)}) copy-start(bf16[1024,512]{1,0:T(8,128)(2,1)} %param.11) | copy-start | bytes 3145732
  6.5 247.6 %reduce-scatter.2.cloned.1.call-start = ((), (), s32[]{:S(2)}) async-start(), calls=%async_computation.2 | async-start | bytes 20971520 | tf_op jit(solution)/shard_map/reduce_scatter | solution.py:31
  6.5 7.9 %copy-start.1 = (s32[1,1,4,2]{2,3,1,0:T(2,128)S(1)}, s32[1,1,4,2]{2,3,1,0:T(2,128)}, u32[]{:S(2)}) copy-start(s32[1,1,4,2]{2,3,1,0:T(2,128)} %param.9) | copy-start | bytes 100
Sparse Core Ops, SparseCore 0:
  50.0 204.1 reduce-scatter.1
where the time goes:
time: 329 us
  waiting for transfers between devices  204 us (62%)
  blocking collectives  61.7 us (19%)
  local copies, waits for them, and re-layouts  28.5 us (9%)
  matrix products  15.9 us (5%)
  between operations  13.4 us (4%)
    reduce_scatter x1, waiting for transfers between devices, local(): lax.psum_scatter(sketch, 'grp', scatter_dimension=0, tiled=True)  204 us
    all_to_all x1, blocking collectives, local(): lax.all_to_all(reduced, 'slab', split_axis=2, concat_axis=1, tiled=True)  61.7 us
    while x1, local copies, waits for them, and re-layouts, local(): sketch = lax.fori_loop(0, live_count, own_step, empty_sketch)  17.7 us
    dot_general x1, matrix products, contract(): jnp.einsum('ias,ar->sir', after_third, second_rows, preferred_element_typ...  14.6 us
    broadcast_in_dim x1, local copies, waits for them, and re-layouts, local(): jnp.zeros((omega3.shape[1], slab_depth, sketch_width), jnp.float32)  7.86 us
  transfers between devices with their start and end apart: 1, of which 1 were waited for; matrix products, arithmetic and copies ran while one was open for 0% of the time, Pallas kernels for 0%

commit v1 on v0

--- a/solution.py
+++ b/solution.py
@@ -29,7 +29,10 @@
 
     sketch = lax.fori_loop(0, live_count, own_step, empty_sketch)
     reduced = lax.psum_scatter(sketch, "grp", scatter_dimension=0, tiled=True).astype(jnp.bfloat16)
-    folded = lax.all_to_all(reduced, "slab", split_axis=2, concat_axis=1, tiled=True)
+    folded = jnp.concatenate(
+        lax.all_to_all(jnp.stack(jnp.split(reduced, lax.axis_size("slab"), axis=2)), "slab", 0, 0),
+        axis=1,
+    )
     return jnp.einsum("ir,sip->rps", omega1, folded, preferred_element_type=jnp.float32)
 
 

time: 329 us -> 313 us (0.951)
  local copies, waits for them, and re-layouts: 28.5 us -> 11.6 us
    while x1 -> x0, local copies, waits for them, and re-layouts: 17.7 us -> none  [local(): sketch = lax.fori_loop(0, live_count, own_step, empty_sketch)]
where the time goes in v1:
time: 313 us
  waiting for transfers between devices  205 us (65%)
  blocking collectives  61.7 us (20%)
  matrix products  15.9 us (5%)
  between operations  13.7 us (4%)
  local copies, waits for them, and re-layouts  11.6 us (4%)
    reduce_scatter x1, waiting for transfers between devices, local(): lax.psum_scatter(sketch, 'grp', scatter_dimension=0, tiled=True)  205 us
    all_to_all x1, blocking collectives, local(): lax.all_to_all(jnp.stack(jnp.split(reduced, lax.axis_size('slab'), axis=2...  61.7 us
    dot_general x1, matrix products, contract(): jnp.einsum('ias,ar->sir', after_third, second_rows, preferred_element_typ...  14.7 us
    broadcast_in_dim x1, local copies, waits for them, and re-layouts, local(): jnp.zeros((omega3.shape[1], slab_depth, sketch_width), jnp.float32)  7.87 us
  transfers between devices with their start and end apart: 1, of which 1 were waited for; matrix products, arithmetic and copies ran while one was open for 0% of the time, Pallas kernels for 0%

profile of v1, /device:TPU:1, one launch (start us, length us, event | category | flops | bytes accessed | tf_op | source)
XLA Modules:
  0.0 313.1 jit_solution(9054220355044883338)
XLA Ops:
  6.5 0.0 copy-start
  6.5 0.0 reduce-scatter.2.cloned.1.call-start
  6.5 0.0 copy-start.1
  6.5 7.9 %broadcast_in_dim.3 = f32[512,16,512]{0,2,1:T(8,128)} broadcast(f32[]{:T(128)} %constant.15.clone.1), dimensions={} | broadcast | bytes 16777220 | tf_op jit(solution)/shard_map/broadcast_in_dim | solution.py:25
  14.4 0.0 copy-done.1
  14.4 18.0 %while.10 = (s32[]{:T(128)}, f32[512,16,512]{0,2,1:T(8,128)}, s32[]{:T(128)}, s32[4,2]{0,1:T(2,128)S(1)}, bf16[2048,512]{1,0:T(8,128)(2,1)}, /*index=5*/bf16[4,1...) while((s32[]{:T(128)}, f32[512,16,512]{0,2,1:T(8,128)}, ...), condition=%wide.region_1.0_spmd, body=%wide.region_0.0_spmd.sunk | while | flops 1347420160 | bytes 34341160 | solution.py:30
  15.1 0.1 constant_dynamic-slice_fusion.2
  15.2 0.6 fusion.31
  17.1 14.7 %bitcast_add_fusion.2 = f32[512,16,512]{0,2,1:T(8,128)} fusion(f32[512,16,512]{0,2,1:T(8,128)} %get-tuple-element.135, bf16[4,16,128,128]{3,2,1,0:T(8,128)(2,1)} %get-tuple-element.151, s32[]{:T(128)S(6)} %select_n.13, bf16[2048,512]{1,0:T(8,128)(2,1)} %get-tuple-element.152, s32[]{:T(128)S(6)} %select_n.14, bf16[2048,512]{1,0:T(8,128)(2,1)} %get-tuple-element.150, ...), kind=kOutput, calls=%fused_computation.clone.1 | convolution fusion | flops 1347420160 | bytes 34340876 | tf_op jit(solution)/shard_map/while/body/ias,ar->sir/dot_general | solution.py:14
  32.4 0.0 reduce-scatter.2.cloned.1.call-update
  32.4 204.9 %reduce-scatter.2.cloned.1.call-done = f32[128,16,512]{0,2,1:T(8,128)} async-done(((f32[512,16,512]{0,2,1:T(8,128)}), f32[128,16,512]{0,2,1:T(8,128)}) %reduce-scatter.2.cloned.1.call-update) | async-done | bytes 4194320 | tf_op jit(solution)/shard_map/reduce_scatter | solution.py:31
  237.3 2.6 convert_element_type.6
  241.4 61.7 %all_to_all.5 = bf16[64,128,16,8]{1,3,2,0:T(8,128)(2,1)S(1)} all-to-all(bf16[64,128,16,8]{1,3,2,0:T(8,128)(2,1)S(1)} %constant_dynamic-update-slice_fusion), channel_id=1, replica_groups=mesh['slab'=64,'grp'=4] {'slab'}, dimensions={0} | all-to-all | bytes 4194304 | tf_op jit(solution)/shard_map/all_to_all | solution.py:33
  303.1 0.0 copy-done
  303.1 1.3 fusion.17
  304.4 1.8 copy.12
  (64 shorter events, 1.2 us)
Async XLA Ops:
  6.5 296.6 %copy-start = (bf16[1024,512]{1,0:T(8,128)(2,1)S(1)}, bf16[1024,512]{1,0:T(8,128)(2,1)}, u32[]{:S(2)}) copy-start(bf16[1024,512]{1,0:T(8,128)(2,1)} %param.11) | copy-start | bytes 3145732
  6.5 230.7 %reduce-scatter.2.cloned.1.call-start = ((), (), s32[]{:S(2)}) async-start(), calls=%async_computation.2 | async-start | bytes 20971520 | tf_op jit(solution)/shard_map/reduce_scatter | solution.py:31
  6.5 7.9 %copy-start.1 = (s32[1,1,4,2]{2,3,1,0:T(2,128)S(1)}, s32[1,1,4,2]{2,3,1,0:T(2,128)}, u32[]{:S(2)}) copy-start(s32[1,1,4,2]{2,3,1,0:T(2,128)} %param.9) | copy-start | bytes 100
Sparse Core Ops, SparseCore 0:
  32.5 204.6 reduce-scatter.1
